TPU v7x, 512 devices: a whole 4x8x8 slice. The times are simulated.
512 devices in a mesh: ctx: 16 (over z_hi, x), tp: 8 (over y), dp: 4 (over z_lo, core).
Axes of the slice: x: 4, y: 8, z: 8 (z_hi: 4, z_lo: 2; z = z_hi * 2 + z_lo), core: 2. Of those that a mesh axis runs over, the one named last changes fastest.
Arguments:
- q_raw: bfloat16 [4, 2048, 2048], P('dp', 'ctx', 'tp'), may hold values from -60 to 60
- k_raw: bfloat16 [4, 2048, 2048], P('dp', 'ctx', 'tp'), may hold values from -60 to 60
- value: bfloat16 [4, 2048, 2048], P('dp', 'ctx', 'tp'), may hold values from -6 to 6
- d_out: bfloat16 [4, 2048, 2048], P('dp', 'ctx', 'tp'), may hold values from -6 to 6
- q_gain: float32 [128], replicated, may hold values from 1.3 to 5
- k_gain: float32 [128], replicated, may hold values from 1.3 to 5
Outputs:
- q_raw_grad: bfloat16 [4, 2048, 2048], P('dp', 'ctx', 'tp')
- k_raw_grad: bfloat16 [4, 2048, 2048], P('dp', 'ctx', 'tp')
- value_grad: bfloat16 [4, 2048, 2048], P('dp', 'ctx', 'tp')
- q_gain_grad: float32 [128], replicated
- k_gain_grad: float32 [128], replicated
All inputs are finite; a program needn't handle non-finite values.
Results may differ from a plain program's by a relative error of at most 0.028.
The roundings to bfloat16 on the way count: a program that leaves them out, or rounds other values in their place, can miss the bound.
Values may be sent and summed in bfloat16 or wider, within the bound.
A program may use at most 64 MiB of HBM per device.

v0:
```python
import math
import jax
import jax.numpy as jnp
from jax import lax
from jax.sharding import PartitionSpec as P

EPSILON = 1e-06


def normalize(raw, gain, heads_here):
    rows = raw.shape[0]
    width = gain.shape[0]
    values = raw.astype(jnp.float32).reshape(rows, heads_here, width)
    inverse = lax.rsqrt(jnp.mean(values * values, axis=2, keepdims=True) + EPSILON)
    unit = values * inverse
    return (unit, inverse, (unit * gain).astype(jnp.bfloat16))


def restore(grad_normed, unit, inverse, gain):
    scaled = grad_normed * gain
    back = inverse * (scaled - unit * jnp.mean(scaled * unit, axis=2, keepdims=True))
    return (back, jnp.sum(grad_normed * unit, axis=(0, 1)))


def block_weights(query_normed, query_out, log_total, delta, key_normed, key_value_pair, scale):
    scores = (
        jnp.einsum("qhd,khd->hqk", query_normed, key_normed, preferred_element_type=jnp.float32)
        * scale
    )
    prob = jnp.exp(scores - log_total[:, :, None])
    dprob = jnp.einsum(
        "qhd,khd->hqk", query_out, key_value_pair, preferred_element_type=jnp.float32
    )
    prob_low = prob.astype(jnp.bfloat16)
    dscore = (prob * (dprob - delta[:, :, None]) * scale).astype(jnp.bfloat16)
    return (prob_low, dscore)


def key_block_terms(query_normed, query_out, log_total, delta, key_normed, key_value_pair, scale):
    prob_low, dscore = block_weights(
        query_normed, query_out, log_total, delta, key_normed, key_value_pair, scale
    )
    dkey = jnp.einsum("hqk,qhd->khd", dscore, query_normed, preferred_element_type=jnp.float32)
    dval = jnp.einsum("hqk,qhd->khd", prob_low, query_out, preferred_element_type=jnp.float32)
    return (dkey, dval)


def local(q_raw, k_raw, value, d_out, q_gain, k_gain):
    width = q_gain.shape[0]
    rows = q_raw.shape[1]
    heads_here = q_raw.shape[2] // width
    flat = heads_here * width
    scale = width ** (-0.5)
    q_unit, q_inverse, q_normed = normalize(q_raw[0], q_gain, heads_here)
    k_unit, k_inverse, k_normed = normalize(k_raw[0], k_gain, heads_here)
    own_value = value[0]
    own_out_flat = d_out[0]
    own_out = own_out_flat.reshape(rows, heads_here, width)
    all_keys, all_values = (
        lax.all_gather(k_normed.reshape(rows, flat), "ctx", axis=0, tiled=True),
        lax.all_gather(own_value, "ctx", axis=0, tiled=True),
    )
    length = all_keys.shape[0]
    block = min(512, length)
    block_count = length // block

    def key_slice(begin, size):
        keys = lax.dynamic_slice_in_dim(all_keys, begin, size, 0).reshape(size, heads_here, width)
        vals = lax.dynamic_slice_in_dim(all_values, begin, size, 0).reshape(size, heads_here, width)
        return (keys, vals)

    def statistics(index, carry):
        top, total, weighted = carry
        keys, vals = key_slice(index * block, block)
        scores = (
            jnp.einsum("qhd,khd->hqk", q_normed, keys, preferred_element_type=jnp.float32) * scale
        )
        dprob = jnp.einsum("qhd,khd->hqk", own_out, vals, preferred_element_type=jnp.float32)
        new_top = jnp.maximum(top, jnp.max(scores, axis=2))
        factor = jnp.exp(top - new_top)
        expo = jnp.exp(scores - new_top[:, :, None])
        return (
            new_top,
            total * factor + jnp.sum(expo, axis=2),
            weighted * factor + jnp.sum(expo * dprob, axis=2),
        )

    start_top = jnp.full((heads_here, rows), -jnp.inf, jnp.float32)
    zero_stat = jnp.zeros((heads_here, rows), jnp.float32)
    top, total, weighted = lax.fori_loop(
        0, block_count, statistics, (start_top, zero_stat, zero_stat)
    )
    log_total = top + jnp.log(total)
    delta = weighted / total

    def query_pass(index, acc):
        keys, vals = key_slice(index * block, block)
        prob_low, dscore = block_weights(q_normed, own_out, log_total, delta, keys, vals, scale)
        return acc + jnp.einsum("hqk,khd->qhd", dscore, keys, preferred_element_type=jnp.float32)

    dq_normed = lax.fori_loop(
        0, block_count, query_pass, jnp.zeros((rows, heads_here, width), jnp.float32)
    )
    dq_back, q_gain_part = restore(dq_normed, q_unit, q_inverse, q_gain)
    size = math.gcd(lax.axis_size("ctx") * rows, 512)

    def one_block(index):
        keys, vals = key_slice(index * size, size)
        dkey, dval = key_block_terms(q_normed, own_out, log_total, delta, keys, vals, scale)
        return jnp.concatenate([dkey.reshape(size, flat), dval.reshape(size, flat)], axis=1)

    summed = lax.psum_scatter(
        lax.map(one_block, jnp.arange(lax.axis_size("ctx") * rows // size))
        .reshape(lax.axis_size("ctx") * rows, 2 * flat)
        .astype(jnp.bfloat16),
        "ctx",
        scatter_dimension=0,
        tiled=True,
    ).astype(jnp.float32)
    dk_normed = summed[:, :flat]
    dv_sum = summed[:, flat:]
    dk_back, k_gain_part = restore(
        dk_normed.reshape(rows, heads_here, width), k_unit, k_inverse, k_gain
    )
    q_gain_total, k_gain_total = lax.psum((q_gain_part, k_gain_part), ("ctx", "tp", "dp"))
    q_grad = dq_back.reshape(rows, flat).astype(jnp.bfloat16)[None]
    k_grad = dk_back.reshape(rows, flat).astype(jnp.bfloat16)[None]
    value_grad = dv_sum.astype(jnp.bfloat16)[None]
    return (q_grad, k_grad, value_grad, q_gain_total / length, k_gain_total / length)


def solution(mesh):
    return jax.shard_map(
        local,
        mesh=mesh,
        in_specs=(
            P("dp", "ctx", "tp"),
            P("dp", "ctx", "tp"),
            P("dp", "ctx", "tp"),
            P("dp", "ctx", "tp"),
            P(),
            P(),
        ),
        out_specs=(P("dp", "ctx", "tp"), P("dp", "ctx", "tp"), P("dp", "ctx", "tp"), P(), P()),
        check_vma=False,
    )
```

profile of v0, /device:TPU:1, one launch (start us, length us, event | category | flops | bytes accessed | tf_op | source)
XLA Modules:
  0.0 363.0 jit_solution(17884126247453620999)
XLA Ops:
  9.2 1.5 multiply_convert_fusion.2
  10.8 1.6 copy.113
  15.4 59.9 %all-gather.4.cloned.1.call-done = bf16[2048,256]{1,0:T(8,128)(2,1)} async-done(((bf16[128,256]{1,0:T(8,128)(2,1)}), bf16[2048,256]{1,0:T(8,128)(2,1)}) %all-gather.4.cloned.1.call-update) | async-done | bytes 1048592 | tf_op jit(solution)/shard_map/all_gather | solution.py:60
  75.4 1.5 copy.118
  76.9 60.4 %all-gather.6.cloned.1.call-done = bf16[1,2048,256]{1,2,0:T(8,128)(2,1)} async-done(((bf16[1,128,256]{1,2,0:T(8,128)(2,1)}), bf16[1,2048,256]{1,2,0:T(8,128)(2,1)}) %all-gather.6.cloned.1.call-update) | async-done | bytes 1048592 | tf_op jit(solution)/shard_map/all_gather | solution.py:61
  137.3 7.0 %while.43 = (s32[]{:T(128)}, f32[2,128]{1,0:T(2,128)S(1)}, f32[2,128]{1,0:T(2,128)S(1)}, f32[2,128]{1,0:T(2,128)S(1)}, bf16[2048,256]{0,1:T(8,128)(2,1)S(1)}, /*...) while((s32[]{:T(128)}, f32[2,128]{1,0:T(2,128)S(1)}, ...), condition=%wide.region_6.0_spmd.clone, body=%wide.region_2.0_spmd.clone.sunk | while | flops 68028160 | bytes 3295418 | solution.py:90
  139.0 1.0 constant_dynamic-slice_fusion.10
  140.8 1.0 constant_dynamic-slice_fusion.10
  142.6 1.0 constant_dynamic-slice_fusion.10
  144.3 16.4 %while.42 = (s32[]{:T(128)}, bf16[4,512,512]{1,2,0:T(8,128)(2,1)}, s32[4]{0:T(128)S(1)}, bf16[2048,256]{0,1:T(8,128)(2,1)S(1)}, bf16[128,2,128]{0,2,1:T(8,128)(2...) while((s32[]{:T(128)}, bf16[4,512,512]{1,2,0:T(8,128)(2,1)}, ...), condition=%wide.region_11.12_spmd, body=%wide.region_10.0_spmd.sunk | while | flops 136183808 | bytes 4982983 | solution.py:113
  145.6 1.0 constant_dynamic-slice_fusion.9
  149.7 1.0 constant_dynamic-slice_fusion.9
  153.8 1.0 constant_dynamic-slice_fusion.9
  157.9 1.0 constant_dynamic-slice_fusion.9
  160.8 4.1 %copy.123 = bf16[4,512,512]{2,1,0:T(8,128)(2,1)} copy(bf16[4,512,512]{1,2,0:T(8,128)(2,1)} %get-tuple-element.336) | data formatting | bytes 4194304 | tf_op jit(solution)/shard_map/convert_element_type | solution.py:115
  165.0 7.3 %while.44 = (s32[]{:T(128)}, f32[128,2,128]{0,2,1:T(8,128)S(1)}, bf16[2048,256]{0,1:T(8,128)(2,1)S(1)}, bf16[128,2,128]{2,0,1:T(8,128)(2,1)S(1)}, f32[2,128]{1,0...) while((s32[]{:T(128)}, f32[128,2,128]{0,2,1:T(8,128)S(1)}, ...), condition=%wide.region_8.0_spmd.clone, body=%wide.region_7.0_spmd.clone.sunk | while | flops 101515264 | bytes 3279033 | solution.py:101
  165.0 1.0 constant_dynamic-slice_fusion.11
  166.8 1.0 constant_dynamic-slice_fusion.11
  168.7 1.0 constant_dynamic-slice_fusion.11
  170.5 1.0 constant_dynamic-slice_fusion.11
  173.3 82.7 %reduce-scatter.2.cloned.1.call-done = bf16[128,512]{1,0:T(8,128)(2,1)} async-done(((bf16[2048,512]{1,0:T(8,128)(2,1)}), bf16[128,512]{1,0:T(8,128)(2,1)}) %reduce-scatter.2.cloned.1.call-update) | async-done | bytes 131088 | tf_op jit(solution)/shard_map/reduce_scatter | solution.py:112
  255.9 1.5 slice_bitcast_fusion
  258.1 1.5 multiply_reduce_fusion
  259.7 96.3 %all-reduce = (f32[128]{0:T(128)S(1)}, f32[128]{0:T(128)S(1)}) all-reduce(f32[128]{0:T(128)S(1)} %get-tuple-element.541, f32[128]{0:T(128)S(1)} %bitcast_reduce_fusion), channel_id=1, replica_groups=mesh['ctx'=16,'tp'=8,'dp'=4] {'ctx','tp','dp'}, use_global_device_ids=true, to_apply=%region_15.16 | all-reduce | flops 256 | bytes 2048 | tf_op jit(solution)/shard_map/psum | solution.py:125
  (94 shorter events, 23.9 us)
Async XLA Ops:
  7.2 68.2 %all-gather.4.cloned.1.call-start = ((), (), s32[]{:S(2)}) async-start(), calls=%async_computation.1 | async-start | bytes 1114112 | tf_op jit(solution)/shard_map/all_gather | solution.py:60
  10.7 126.5 %all-gather.6.cloned.1.call-start = ((), (), s32[]{:S(2)}) async-start(), calls=%async_computation.3 | async-start | bytes 1114112 | tf_op jit(solution)/shard_map/all_gather | solution.py:61
  12.4 243.6 %reduce-scatter.2.cloned.1.call-start = ((), (), s32[]{:S(2)}) async-start(), calls=%async_computation.2 | async-start | bytes 2228224 | tf_op jit(solution)/shard_map/reduce_scatter | solution.py:112
  164.9 7.3 %copy-start.1 = (f32[128]{0:T(128)S(1)}, f32[128]{0:T(128)}, u32[]{:S(2)}) copy-start(f32[128]{0:T(128)} %param.16) | copy-start | bytes 1540
  165.0 92.6 %copy-start.2 = (f32[128]{0:T(128)S(1)}, f32[128]{0:T(128)}, u32[]{:S(2)}) copy-start(f32[128]{0:T(128)} %param.17) | copy-start | bytes 1540
  165.0 93.2 %copy-start = (bf16[1,128,256]{2,1,0:T(8,128)(2,1)S(1)}, bf16[1,128,256]{2,1,0:T(8,128)(2,1)}, u32[]{:S(2)}) copy-start(bf16[1,128,256]{2,1,0:T(8,128)(2,1)} %param.13) | copy-start | bytes 196612
Sparse Core Ops, SparseCore 0:
  11.6 63.7 all-gather.3
  78.9 58.3 all-gather.5
  165.1 90.8 reduce-scatter.1
where the time goes:
time: 364 us; the launch traced here: 363 us
  waiting for transfers between devices  203 us (56%)
  blocking collectives  96.3 us (26%)
  local copies, waits for them, and re-layouts  26.5 us (7%)
  between operations  14 us (4%)
  other arithmetic  10.5 us (3%)
  matrix products  9.47 us (3%)
    psum x1, blocking collectives, local(): lax.psum((q_gain_part, k_gain_part), ('ctx', 'tp', 'dp'))  96.3 us
    reduce_scatter x1, waiting for transfers between devices, local(): lax.psum_scatter(lax.map(one_block, jnp.arange(lax.axis_size('ctx') * row...  82.7 us
    all_gather x1, waiting for transfers between devices, local(): lax.all_gather(own_value, 'ctx', axis=0, tiled=True)  60.4 us
    all_gather x1, waiting for transfers between devices, local(): lax.all_gather(k_normed.reshape(rows, flat), 'ctx', axis=0, tiled=True)  59.9 us
    dynamic_slice x12, local copies, waits for them, and re-layouts, key_slice(): lax.dynamic_slice_in_dim(all_values, begin, size, 0)  12 us
  transfers between devices with their start and end apart: 3, of which 3 were waited for; matrix products, arithmetic and copies ran while one was open for 4% of the time, Pallas kernels for 0%

commit v1 on v0

--- a/solution.py
+++ b/solution.py
@@ -5,6 +5,12 @@
 from jax.sharding import PartitionSpec as P
 
 EPSILON = 1e-06
+
+
+def recast_signs(local_block, comm_axis):
+    built = jnp.stack([local_block for _ in range(lax.axis_size(comm_axis))])
+    f_now = lax.all_to_all(built, comm_axis, 0, 0)
+    return jnp.concatenate(f_now, axis=0)
 
 
 def normalize(raw, gain, heads_here):
@@ -57,7 +63,7 @@
     own_out_flat = d_out[0]
     own_out = own_out_flat.reshape(rows, heads_here, width)
     all_keys, all_values = (
-        lax.all_gather(k_normed.reshape(rows, flat), "ctx", axis=0, tiled=True),
+        recast_signs(k_normed.reshape(rows, flat), "ctx"),
         lax.all_gather(own_value, "ctx", axis=0, tiled=True),
     )
     length = all_keys.shape[0]

time: 364 us -> 319 us (0.88)
  waiting for transfers between devices: 203 us -> 148 us
  starting transfers between devices: 0.12 us -> 13.5 us
    all_gather x1 -> x0, waiting for transfers between devices: 59.9 us -> none  [local(): lax.all_gather(k_normed.reshape(rows, flat), 'ctx', axis=0, tiled=True)]
    all_to_all x0 -> x1, waiting for transfers between devices: none -> 20.2 us  [recast_signs(): f_now = lax.all_to_all(built, comm_axis, 0, 0)]
    all_gather x1, waiting for transfers between devices: 60.4 us -> 44.7 us  [local(): lax.all_gather(own_value, 'ctx', axis=0, tiled=True)]
    all_to_all x0 -> x1, starting transfers between devices: none -> 13.4 us  [recast_signs(): f_now = lax.all_to_all(built, comm_axis, 0, 0)]
  transfers between devices with their start and end apart: 3 -> 3, of which waited for: 3 -> 3; matrix products, arithmetic and copies ran while one was open for 4% -> 3% of each run, Pallas kernels for 0% -> 0%
where the time goes in v1:
time: 319 us; the launch traced here: 318 us
  waiting for transfers between devices  148 us (46%)
  blocking collectives  96.2 us (30%)
  local copies, waits for them, and re-layouts  25.1 us (8%)
  between operations  14.3 us (4%)
  starting transfers between devices  13.5 us (4%)
  matrix products  9.48 us (3%)
  other arithmetic  9.27 us (3%)
    psum x1, blocking collectives, local(): lax.psum((q_gain_part, k_gain_part), ('ctx', 'tp', 'dp'))  96.2 us
    reduce_scatter x1, waiting for transfers between devices, local(): lax.psum_scatter(lax.map(one_block, jnp.arange(lax.axis_size('ctx') * row...  82.5 us
    all_gather x1, waiting for transfers between devices, local(): lax.all_gather(own_value, 'ctx', axis=0, tiled=True)  44.7 us
    all_to_all x1, waiting for transfers between devices, recast_signs(): f_now = lax.all_to_all(built, comm_axis, 0, 0)  20.2 us
    all_to_all x1, starting transfers between devices, recast_signs(): f_now = lax.all_to_all(built, comm_axis, 0, 0)  13.4 us
    dynamic_slice x12, local copies, waits for them, and re-layouts, key_slice(): lax.dynamic_slice_in_dim(all_values, begin, size, 0)  12 us
  transfers between devices with their start and end apart: 3, of which 3 were waited for; matrix products, arithmetic and copies ran while one was open for 3% of the time, Pallas kernels for 0%

profile of v1, /device:TPU:1, one launch (start us, length us, event | category | flops | bytes accessed | tf_op | source)
XLA Modules:
  0.0 318.4 jit_solution(3728979152250896261)
XLA Ops:
  10.3 1.2 stack.3
  11.5 13.4 %all-to-all-start = ((bf16[16,128,256]{1,2,0:T(8,128)(2,1)}), bf16[16,128,256]{1,2,0:T(8,128)(2,1)S(1)}, u32[]{:S(2)}, u32[]{:S(2)}) async-start(bf16[16,128,256]{1,2,0:T(8,128)(2,1)} %stack.3), calls=%async_computation | async-start | bytes 2097152 | tf_op jit(solution)/shard_map/all_to_all | solution.py:12
  26.5 20.2 %all-to-all-done = bf16[16,128,256]{1,2,0:T(8,128)(2,1)S(1)} async-done(((bf16[16,128,256]{1,2,0:T(8,128)(2,1)}), bf16[16,128,256]{1,2,0:T(8,128)(2,1)S(1)}, u32[]{:S(2)}, u32[]{:S(2)}) %all-to-all-start) | async-done | bytes 1048608 | tf_op jit(solution)/shard_map/all_to_all | solution.py:12
  48.0 44.7 %all-gather.3.cloned.1.call-done = bf16[1,2048,256]{1,2,0:T(8,128)(2,1)} async-done(((bf16[1,128,256]{1,2,0:T(8,128)(2,1)}), bf16[1,2048,256]{1,2,0:T(8,128)(2,1)}) %all-gather.3.cloned.1.call-update) | async-done | bytes 1048592 | tf_op jit(solution)/shard_map/all_gather | solution.py:67
  92.7 7.0 %while.43 = (s32[]{:T(128)}, f32[2,128]{1,0:T(2,128)S(1)}, f32[2,128]{1,0:T(2,128)S(1)}, f32[2,128]{1,0:T(2,128)S(1)}, bf16[2048,256]{0,1:T(8,128)(2,1)S(1)}, /*...) while((s32[]{:T(128)}, f32[2,128]{1,0:T(2,128)S(1)}, ...), condition=%wide.region_6.0_spmd.clone, body=%wide.region_2.0_spmd.clone.sunk | while | flops 68028160 | bytes 3295418 | solution.py:96
  92.7 1.0 constant_dynamic-slice_fusion.10
  94.4 1.0 constant_dynamic-slice_fusion.10
  96.2 1.0 constant_dynamic-slice_fusion.10
  98.0 1.0 constant_dynamic-slice_fusion.10
  99.7 16.4 %while.42 = (s32[]{:T(128)}, bf16[4,512,512]{1,2,0:T(8,128)(2,1)}, s32[4]{0:T(128)S(1)}, bf16[2048,256]{0,1:T(8,128)(2,1)S(1)}, bf16[128,2,128]{0,2,1:T(8,128)(2...) while((s32[]{:T(128)}, bf16[4,512,512]{1,2,0:T(8,128)(2,1)}, ...), condition=%wide.region_11.12_spmd, body=%wide.region_10.0_spmd.sunk | while | flops 136183808 | bytes 4982983 | solution.py:119
  101.0 1.0 constant_dynamic-slice_fusion.9
  105.1 1.0 constant_dynamic-slice_fusion.9
  109.2 1.0 constant_dynamic-slice_fusion.9
  113.3 1.0 constant_dynamic-slice_fusion.9
  116.2 4.1 %copy.130 = bf16[4,512,512]{2,1,0:T(8,128)(2,1)} copy(bf16[4,512,512]{1,2,0:T(8,128)(2,1)} %get-tuple-element.336) | data formatting | bytes 4194304 | tf_op jit(solution)/shard_map/convert_element_type | solution.py:121
  120.4 7.3 %while.44 = (s32[]{:T(128)}, f32[128,2,128]{0,2,1:T(8,128)S(1)}, bf16[2048,256]{0,1:T(8,128)(2,1)S(1)}, bf16[128,2,128]{2,0,1:T(8,128)(2,1)S(1)}, f32[2,128]{1,0...) while((s32[]{:T(128)}, f32[128,2,128]{0,2,1:T(8,128)S(1)}, ...), condition=%wide.region_8.0_spmd.clone, body=%wide.region_7.0_spmd.clone.sunk | while | flops 101515264 | bytes 3279033 | solution.py:107
  120.4 1.0 constant_dynamic-slice_fusion.11
  122.2 1.0 constant_dynamic-slice_fusion.11
  124.0 1.0 constant_dynamic-slice_fusion.11
  125.8 1.0 constant_dynamic-slice_fusion.11
  128.6 82.5 %reduce-scatter.2.cloned.1.call-done = bf16[128,512]{1,0:T(8,128)(2,1)} async-done(((bf16[2048,512]{1,0:T(8,128)(2,1)}), bf16[128,512]{1,0:T(8,128)(2,1)}) %reduce-scatter.2.cloned.1.call-update) | async-done | bytes 131088 | tf_op jit(solution)/shard_map/reduce_scatter | solution.py:118
  211.2 1.5 slice_bitcast_fusion
  213.3 1.5 multiply_reduce_fusion
  214.9 96.2 %all-reduce = (f32[128]{0:T(128)S(1)}, f32[128]{0:T(128)S(1)}) all-reduce(f32[128]{0:T(128)S(1)} %get-tuple-element.541, f32[128]{0:T(128)S(1)} %bitcast_reduce_fusion), channel_id=1, replica_groups=mesh['ctx'=16,'tp'=8,'dp'=4] {'ctx','tp','dp'}, use_global_device_ids=true, to_apply=%region_15.16 | all-reduce | flops 256 | bytes 2048 | tf_op jit(solution)/shard_map/psum | solution.py:131
  (103 shorter events, 23.6 us)
Async XLA Ops:
  8.9 16.1 %copy-start.2 = (bf16[1,128,256]{2,1,0:T(8,128)(2,1)S(1)}, bf16[1,128,256]{2,1,0:T(8,128)(2,1)}, u32[]{:S(2)}) copy-start(bf16[1,128,256]{2,1,0:T(8,128)(2,1)} %param.14) | copy-start | bytes 196612
  9.0 16.9 %copy-start.3 = (bf16[1,128,256]{2,1,0:T(8,128)(2,1)S(1)}, bf16[1,128,256]{2,1,0:T(8,128)(2,1)}, u32[]{:S(2)}) copy-start(bf16[1,128,256]{2,1,0:T(8,128)(2,1)} %param.15) | copy-start | bytes 196612
  9.3 16.8 %copy-start.1 = (bf16[1,128,256]{2,1,0:T(8,128)(2,1)S(1)}, bf16[1,128,256]{2,1,0:T(8,128)(2,1)}, u32[]{:S(2)}) copy-start(bf16[1,128,256]{2,1,0:T(8,128)(2,1)} %param.12) | copy-start | bytes 196612
  10.2 16.1 %copy-start.4 = (f32[128]{0:T(128)S(1)}, f32[128]{0:T(128)}, u32[]{:S(2)}) copy-start(f32[128]{0:T(128)} %param.16) | copy-start | bytes 1540
  11.5 35.2 %all-to-all-start = ((bf16[16,128,256]{1,2,0:T(8,128)(2,1)}), bf16[16,128,256]{1,2,0:T(8,128)(2,1)S(1)}, u32[]{:S(2)}, u32[]{:S(2)}) async-start(bf16[16,128,256]{1,2,0:T(8,128)(2,1)} %stack.3), calls=%async_computation | async-start | bytes 2097152 | tf_op jit(solution)/shard_map/all_to_all | solution.py:12
  25.0 67.7 %all-gather.3.cloned.1.call-start = ((), (), s32[]{:S(2)}) async-start(), calls=%async_computation.3 | async-start | bytes 1114112 | tf_op jit(solution)/shard_map/all_gather | solution.py:67
  25.8 185.4 %reduce-scatter.2.cloned.1.call-start = ((), (), s32[]{:S(2)}) async-start(), calls=%async_computation.2 | async-start | bytes 2228224 | tf_op jit(solution)/shard_map/reduce_scatter | solution.py:118
  120.3 92.4 %copy-start.5 = (f32[128]{0:T(128)S(1)}, f32[128]{0:T(128)}, u32[]{:S(2)}) copy-start(f32[128]{0:T(128)} %param.17) | copy-start | bytes 1540
  120.4 93.0 %copy-start = (bf16[1,128,256]{2,1,0:T(8,128)(2,1)S(1)}, bf16[1,128,256]{2,1,0:T(8,128)(2,1)}, u32[]{:S(2)}) copy-start(bf16[1,128,256]{2,1,0:T(8,128)(2,1)} %param.13) | copy-start | bytes 196612
Sparse Core Ops, SparseCore 0:
  29.4 63.2 all-gather.2
  120.5 90.6 reduce-scatter.1
